TPU v7x, 128 devices: a whole 4x4x4 slice. The times are simulated.
128 devices in a mesh: sx: 16 (over z, y), sy: 8 (over x, core).
Axes of the slice: x: 4, y: 4, z: 4, core: 2. Of those that a mesh axis runs over, the one named last changes fastest.
Arguments:
- obs_values: bfloat16 [32768, 64], P(('sx', 'sy')), may hold values from -6 to 6
- obs_dest: int32 [32768, 1], P(('sx', 'sy')), may hold values from 0 to 127; in each aligned block of 256 rows (0 to 255, 256 to 511, ...) at most 4 rows name the same one
- obs_node: int32 [32768], P(('sx', 'sy')), may hold values from 0 to 2047
- schur: bfloat16 [16, 8, 2048, 2048], P('sx', 'sy'), as said below
- local_inverse: bfloat16 [16, 8, 2048, 2048], P('sx', 'sy'), as said below
- coarse_inverse: float32 [1024, 1024], P(('sx', 'sy')), as said below
Outputs:
- solution_field: float32 [16, 8, 64, 2048], P('sx', 'sy')
- residual: float32 [16, 8, 64, 2048], P('sx', 'sy')
Inputs may be any that keep to these rules, and one draw needn't show every extreme that they name: `obs_dest`: at most 4 observations of one device go to one subdomain. `schur`: symmetric positive definite. `local_inverse`: symmetric positive definite. `coarse_inverse`: symmetric positive definite.
All inputs are finite; a program needn't handle non-finite values.
Results may differ from a plain program's by a relative error of at most 0.04.
Values may be sent and summed in bfloat16 or wider, within the bound.
A program may use at most 128 MiB of HBM per device.

v0:
```python
import jax
import jax.numpy as jnp
from jax import lax
from jax.sharding import PartitionSpec as P

ITERS = 6


def shortened(array):

    def short(part):
        return part.astype(jnp.bfloat16) if part.dtype == jnp.float32 else part

    return jax.tree.map(short, array)


def padded_2(cells, sides, width):
    for axis, dim in sides:
        count = lax.axis_size(axis)
        ends = count - 1
        head = lax.slice_in_dim(cells, 0, width, axis=dim)
        tail = lax.slice_in_dim(cells, cells.shape[dim] - width, cells.shape[dim], axis=dim)
        cells = jnp.concatenate(
            [
                lax.ppermute(tail, axis, [(i, (i + 1) % count) for i in range(ends)]),
                cells,
                lax.ppermute(head, axis, [((i + 1) % count, i) for i in range(ends)]),
            ],
            axis=dim,
        )
    return cells


def edge_weights(size):
    edge_len = size // 4
    col_index = lax.axis_index("sx")
    row_index = lax.axis_index("sy")
    col_count = lax.axis_size("sx")
    row_count = lax.axis_size("sy")
    sides = (
        jnp.where(col_index > 0, 0.5, 1.0),
        jnp.where(col_index < col_count - 1, 0.5, 1.0),
        jnp.where(row_index > 0, 0.5, 1.0),
        jnp.where(row_index < row_count - 1, 0.5, 1.0),
    )
    return jnp.concatenate([jnp.full((edge_len,), value, jnp.float32) for value in sides])


def coarse_basis(size, count):
    edge_len = size // 4
    node = jnp.arange(size)
    side = node // edge_len
    offset = (node % edge_len).astype(jnp.float32) - (edge_len - 1) / 2.0
    norm_ramp = jnp.sqrt(jnp.float32(edge_len * (edge_len * edge_len - 1) / 12.0))
    column = jnp.arange(count)
    on_edge = side[:, None] == (column // 2)[None, :]
    value = jnp.where(
        (column % 2 == 0)[None, :],
        1.0 / jnp.sqrt(jnp.float32(edge_len)),
        offset[:, None] / norm_ramp,
    )
    return jnp.where(on_edge, value, 0.0)


def assemble(local):
    edge_len = local.shape[1] // 4
    west_part = local[:, 0:edge_len]
    east_part = local[:, edge_len : 2 * edge_len]
    south_part = local[:, 2 * edge_len : 3 * edge_len]
    north_part = local[:, 3 * edge_len :]
    padded = padded_2(shortened(local[None, None]), (("sx", 0), ("sy", 1)), 1)
    west = west_part + padded[0, 1, :, edge_len : 2 * edge_len]
    east = east_part + padded[2, 1, :, 0:edge_len]
    south = south_part + padded[1, 0, :, 3 * edge_len :]
    north = north_part + padded[1, 2, :, 2 * edge_len : 3 * edge_len]
    return jnp.concatenate([west, east, south, north], axis=1)


def gather_coarse(coarse_local):
    return lax.all_gather(coarse_local, ("sx", "sy"), axis=0, tiled=True)


def body(obs_values, obs_dest, obs_node, schur, local_inverse, coarse_inverse):
    hp = lax.Precision.HIGHEST
    size = schur.shape[-1]
    count = coarse_inverse.shape[0]
    realiz = obs_values.shape[1]
    obs_count = obs_values.shape[0]
    row_count = lax.axis_size("sy")
    dev_count = lax.axis_size("sx") * row_count
    target = obs_dest[:, 0]
    capacity = max(2, 2 * obs_count // dev_count)
    match_table = (target[:, None] == jnp.arange(dev_count)[None, :]).astype(jnp.int32)
    slot_index = jnp.sum(jnp.cumsum(match_table, axis=0) * match_table, axis=1) - 1
    position = target * capacity + slot_index
    send_values = (
        jnp.zeros((dev_count * capacity, realiz), jnp.bfloat16).at[position].set(obs_values)
    )
    send_nodes = jnp.zeros((dev_count * capacity,), jnp.int32).at[position].set(obs_node)
    got_values, got_nodes = (
        lax.all_to_all(
            send_values.reshape(dev_count, capacity, realiz),
            ("sx", "sy"),
            split_axis=0,
            concat_axis=0,
            tiled=True,
        ),
        lax.all_to_all(
            send_nodes.reshape(dev_count, capacity),
            ("sx", "sy"),
            split_axis=0,
            concat_axis=0,
            tiled=True,
        ),
    )
    load = jax.ops.segment_sum(
        got_values.reshape(-1, realiz).astype(jnp.float32), got_nodes.reshape(-1), num_segments=size
    )
    rhs = assemble(load.T)
    weight = edge_weights(size)[None, :]
    basis = coarse_basis(size, count)
    schur_mat = schur[0, 0]
    inverse_mat = local_inverse[0, 0]

    def project(vec):
        return jnp.dot(weight * vec, basis, precision=hp).T

    def precond(vec, coarse_all):
        scaled = weight * vec
        part = jnp.dot(scaled.astype(jnp.bfloat16), inverse_mat, preferred_element_type=jnp.float32)
        solved = jnp.dot(coarse_inverse, coarse_all, precision=hp)
        correction = jnp.dot(solved.T, basis.T, precision=hp)
        return assemble(weight * (part + correction))

    def products(left, right):
        return lax.psum(jnp.sum(weight * left * right, axis=1), ("sx", "sy"))

    solution_field = jnp.zeros_like(rhs)
    residual = rhs
    coarse_resid = gather_coarse(project(residual))
    precon = precond(residual, coarse_resid)
    direction = precon
    rz_now = products(residual, precon)
    for step in range(ITERS):
        image = assemble(
            jnp.dot(direction.astype(jnp.bfloat16), schur_mat, preferred_element_type=jnp.float32)
        )
        curv_local = jnp.sum(weight * direction * image, axis=1)
        curv = lax.psum(curv_local, ("sx", "sy"))
        alpha = rz_now / curv
        solution_field = solution_field + alpha[:, None] * direction
        residual = residual - alpha[:, None] * image
        if step < ITERS - 1:
            coarse_resid = gather_coarse(project(residual))
            precon = precond(residual, coarse_resid)
            rz_next = products(residual, precon)
            direction = precon + (rz_next / rz_now)[:, None] * direction
            rz_now = rz_next
    return (solution_field[None, None], residual[None, None])


def solution(mesh):
    placed = (
        P(("sx", "sy"), None),
        P(("sx", "sy"), None),
        P(("sx", "sy")),
        P("sx", "sy", None, None),
        P("sx", "sy", None, None),
        P(("sx", "sy"), None),
    )
    return jax.shard_map(
        body,
        mesh=mesh,
        in_specs=placed,
        out_specs=(P("sx", "sy", None, None), P("sx", "sy", None, None)),
        check_vma=False,
    )
```

profile of v0, /device:TPU:1, one launch (start us, length us, event | category | flops | bytes accessed | tf_op | source)
XLA Modules:
  0.0 1432.0 jit_solution(6117860953516433841)
XLA Ops:
  5.6 11.5 all-to-all-start
  32.6 8.1 all-to-all-done.1
  60.7 7.6 collective-permute-done.3
  72.7 39.9 %all_gather.18 = f32[1024,64]{1,0:T(8,128)S(1)} all-gather(f32[8,64]{1,0:T(8,128)S(1)} %fusion.35), channel_id=1, replica_groups=mesh['sx'=16,'sy'=8] {'sx','sy'}, dimensions={0}, use_global_device_ids=true | all-gather | bytes 264192 | tf_op jit(solution)/shard_map/all_gather | solution.py:80
  136.0 7.7 collective-permute-done.7
  163.3 7.7 collective-permute-done.11
  172.5 69.8 %all-reduce = (f32[64]{0:T(128)S(1)}, f32[64]{0:T(128)S(1)}) all-reduce(f32[64]{0:T(128)S(1)} %get-tuple-element.3, f32[64]{0:T(128)S(1)} %get-tuple-element.2), channel_id=1, replica_groups=mesh['sx'=16,'sy'=8] {'sx','sy'}, use_global_device_ids=true, to_apply=%region_7.8 | all-reduce | flops 128 | bytes 1024 | tf_op jit(solution)/shard_map/psum | solution.py:136
  249.8 34.5 %all_gather.19 = f32[1024,64]{1,0:T(8,128)S(1)} all-gather(f32[8,64]{1,0:T(8,128)S(1)} %fusion.34), channel_id=1, replica_groups=mesh['sx'=16,'sy'=8] {'sx','sy'}, dimensions={0}, use_global_device_ids=true | all-gather | bytes 264192 | tf_op jit(solution)/shard_map/all_gather | solution.py:80
  302.5 7.7 collective-permute-done.15
  311.7 67.8 %psum.86 = f32[64]{0:T(128)S(1)} all-reduce(f32[64]{0:T(128)S(1)} %multiply_reduce_fusion.8), channel_id=1, replica_groups=mesh['sx'=16,'sy'=8] {'sx','sy'}, use_global_device_ids=true, to_apply=%region_11.12 | all-reduce | flops 64 | bytes 512 | tf_op jit(solution)/shard_map/psum | solution.py:136
  400.4 7.4 collective-permute-done.19
  409.6 68.1 %psum.87 = f32[64]{0:T(128)S(1)} all-reduce(f32[64]{0:T(128)S(1)} %multiply_reduce_fusion.7), channel_id=1, replica_groups=mesh['sx'=16,'sy'=8] {'sx','sy'}, use_global_device_ids=true, to_apply=%region_13.14 | all-reduce | flops 64 | bytes 512 | tf_op jit(solution)/shard_map/psum | solution.py:149
  485.2 34.6 %all_gather.20 = f32[1024,64]{1,0:T(8,128)S(1)} all-gather(f32[8,64]{1,0:T(8,128)S(1)} %fusion.33), channel_id=1, replica_groups=mesh['sx'=16,'sy'=8] {'sx','sy'}, dimensions={0}, use_global_device_ids=true | all-gather | bytes 264192 | tf_op jit(solution)/shard_map/all_gather | solution.py:80
  538.0 7.7 collective-permute-done.23
  547.9 68.0 %psum.88 = f32[64]{0:T(128)S(1)} all-reduce(f32[64]{0:T(128)S(1)} %multiply_reduce_fusion.6), channel_id=1, replica_groups=mesh['sx'=16,'sy'=8] {'sx','sy'}, use_global_device_ids=true, to_apply=%region_15.16 | all-reduce | flops 64 | bytes 512 | tf_op jit(solution)/shard_map/psum | solution.py:136
  637.8 7.3 collective-permute-done.27
  647.0 68.1 %psum.89 = f32[64]{0:T(128)S(1)} all-reduce(f32[64]{0:T(128)S(1)} %multiply_reduce_fusion.5), channel_id=1, replica_groups=mesh['sx'=16,'sy'=8] {'sx','sy'}, use_global_device_ids=true, to_apply=%region_17.18 | all-reduce | flops 64 | bytes 512 | tf_op jit(solution)/shard_map/psum | solution.py:149
  723.6 34.8 %all_gather.21 = f32[1024,64]{1,0:T(8,128)S(1)} all-gather(f32[8,64]{1,0:T(8,128)S(1)} %fusion.32), channel_id=1, replica_groups=mesh['sx'=16,'sy'=8] {'sx','sy'}, dimensions={0}, use_global_device_ids=true | all-gather | bytes 264192 | tf_op jit(solution)/shard_map/all_gather | solution.py:80
  776.6 7.7 collective-permute-done.31
  785.8 68.0 %psum.90 = f32[64]{0:T(128)S(1)} all-reduce(f32[64]{0:T(128)S(1)} %multiply_reduce_fusion.4), channel_id=1, replica_groups=mesh['sx'=16,'sy'=8] {'sx','sy'}, use_global_device_ids=true, to_apply=%region_19.20 | all-reduce | flops 64 | bytes 512 | tf_op jit(solution)/shard_map/psum | solution.py:136
  874.7 7.3 collective-permute-done.35
  883.9 68.1 %psum.91 = f32[64]{0:T(128)S(1)} all-reduce(f32[64]{0:T(128)S(1)} %multiply_reduce_fusion.3), channel_id=1, replica_groups=mesh['sx'=16,'sy'=8] {'sx','sy'}, use_global_device_ids=true, to_apply=%region_21.22 | all-reduce | flops 64 | bytes 512 | tf_op jit(solution)/shard_map/psum | solution.py:149
  959.4 34.5 %all_gather.22 = f32[1024,64]{1,0:T(8,128)S(1)} all-gather(f32[8,64]{1,0:T(8,128)S(1)} %fusion.31), channel_id=1, replica_groups=mesh['sx'=16,'sy'=8] {'sx','sy'}, dimensions={0}, use_global_device_ids=true | all-gather | bytes 264192 | tf_op jit(solution)/shard_map/all_gather | solution.py:80
  1012.2 7.7 collective-permute-done.39
  1022.2 68.0 %psum.92 = f32[64]{0:T(128)S(1)} all-reduce(f32[64]{0:T(128)S(1)} %multiply_reduce_fusion.2), channel_id=1, replica_groups=mesh['sx'=16,'sy'=8] {'sx','sy'}, use_global_device_ids=true, to_apply=%region_23.24 | all-reduce | flops 64 | bytes 512 | tf_op jit(solution)/shard_map/psum | solution.py:136
  1112.1 7.3 collective-permute-done.43
  1121.3 68.1 %psum.93 = f32[64]{0:T(128)S(1)} all-reduce(f32[64]{0:T(128)S(1)} %multiply_reduce_fusion.1), channel_id=1, replica_groups=mesh['sx'=16,'sy'=8] {'sx','sy'}, use_global_device_ids=true, to_apply=%region_25.26 | all-reduce | flops 64 | bytes 512 | tf_op jit(solution)/shard_map/psum | solution.py:149
  1196.8 34.6 %all_gather.23 = f32[1024,64]{1,0:T(8,128)S(1)} all-gather(f32[8,64]{1,0:T(8,128)S(1)} %fusion.30), channel_id=1, replica_groups=mesh['sx'=16,'sy'=8] {'sx','sy'}, dimensions={0}, use_global_device_ids=true | all-gather | bytes 264192 | tf_op jit(solution)/shard_map/all_gather | solution.py:80
  1249.6 7.7 collective-permute-done.47
  1258.8 68.0 %psum.94 = f32[64]{0:T(128)S(1)} all-reduce(f32[64]{0:T(128)S(1)} %multiply_reduce_fusion), channel_id=1, replica_groups=mesh['sx'=16,'sy'=8] {'sx','sy'}, use_global_device_ids=true, to_apply=%region_27.28 | all-reduce | flops 64 | bytes 512 | tf_op jit(solution)/shard_map/psum | solution.py:136
  1347.6 7.3 collective-permute-done.51
  1357.7 68.1 %psum.95 = f32[64]{0:T(128)S(1)} all-reduce(f32[64]{0:T(128)S(1)} %fusion.48), channel_id=1, replica_groups=mesh['sx'=16,'sy'=8] {'sx','sy'}, use_global_device_ids=true, to_apply=%region_29.30 | all-reduce | flops 64 | bytes 512 | tf_op jit(solution)/shard_map/psum | solution.py:149
  (316 shorter events, 348.6 us)
Async XLA Ops:
  5.6 21.0 %all-to-all-start = ((s32[128,1,4]{2,1,0:T(1,128)}), s32[128,1,4]{2,1,0:T(1,128)S(1)}, u32[]{:S(2)}, u32[]{:S(2)}) async-start(s32[128,1,4]{2,1,0:T(1,128)} %bitcast.7), calls=%async_computation | async-start | bytes 131072 | tf_op jit(solution)/shard_map/all_to_all | solution.py:108
  26.6 14.0 all-to-all-start.1
  53.7 14.6 %collective-permute-start.3 = (bf16[3,1,64,2048]{3,2,1,0:T(8,128)(2,1)S(1)}, bf16[3,1,64,2048]{3,2,1,0:T(8,128)(2,1)S(1)}, u32[]{:S(2)}, u32[]{:S(2)}) collective-permute-start(bf16[3,1,64,2048]{3,2,1,0:T(8,128)(2,1)S(1)} %pad_maximum_fusion), channel_id=1, source_target_pairs={{1,0},{2,1},{3,2},{4,3},{5,4},{6,5},{7,6},{9,8},{10,9},{11,10},{12... | collective-permute-start | bytes 2359304 | tf_op jit(solution)/shard_map/ppermute | solution.py:27
  57.6 11.9 collective-permute-start.2
  119.8 9.6 collective-permute-start.5
  130.4 13.3 collective-permute-start.7
  133.6 11.3 collective-permute-start.6
  156.1 15.0 %collective-permute-start.11 = (bf16[3,1,64,2048]{3,2,1,0:T(8,128)(2,1)S(1)}, bf16[3,1,64,2048]{3,2,1,0:T(8,128)(2,1)S(1)}, u32[]{:S(2)}, u32[]{:S(2)}) collective-permute-start(bf16[3,1,64,2048]{3,2,1,0:T(8,128)(2,1)S(1)} %pad_maximum_fusion.2), channel_id=1, source_target_pairs={{1,0},{2,1},{3,2},{4,3},{5,4},{6,5},{7,6},{9,8},{10,9},{11,10},{12... | collective-permute-start | bytes 2359304 | tf_op jit(solution)/shard_map/ppermute | solution.py:27
  158.0 14.2 collective-permute-start.10
  286.4 9.6 collective-permute-start.13
  297.0 13.3 collective-permute-start.15
  300.2 11.3 collective-permute-start.14
  394.3 13.5 collective-permute-start.19
  398.5 10.8 collective-permute-start.18
  521.8 9.6 collective-permute-start.21
  532.4 13.3 collective-permute-start.23
  535.6 11.3 collective-permute-start.22
  631.7 13.4 collective-permute-start.27
  635.9 10.8 collective-permute-start.26
  771.0 13.3 collective-permute-start.31
  774.2 11.3 collective-permute-start.30
  868.5 13.4 collective-permute-start.35
  872.8 10.8 collective-permute-start.34
  996.0 9.6 collective-permute-start.37
  1006.6 13.3 collective-permute-start.39
  1009.8 11.3 collective-permute-start.38
  1106.0 13.4 collective-permute-start.43
  1110.2 10.8 collective-permute-start.42
  1244.0 13.3 collective-permute-start.47
  1247.2 11.3 collective-permute-start.46
  1341.5 13.5 collective-permute-start.51
  1345.7 10.8 collective-permute-start.50
  (67 other events, 2812.2 us)
where the time goes:
time: 1440 us; the launch traced here: 1430 us
  blocking collectives  963 us (67%)
  waiting for transfers between devices  190 us (13%)
  starting transfers between devices  164 us (11%)
  matrix products  82.1 us (6%)
  other arithmetic  20.9 us (1%)
    psum x6, blocking collectives, products(): return lax.psum(jnp.sum(weight * left * right, axis=1), ('sx', 'sy'))  410 us
    psum x5, blocking collectives, body(): curv = lax.psum(curv_local, ('sx', 'sy'))  340 us
    all_gather x6, blocking collectives, gather_coarse(): return lax.all_gather(coarse_local, ('sx', 'sy'), axis=0, tiled=True)  213 us
    ppermute x26, waiting for transfers between devices, padded_2(): lax.ppermute(head, axis, [((i + 1) % count, i) for i in range(ends)])  146 us
    ppermute x26, starting transfers between devices, padded_2(): lax.ppermute(tail, axis, [(i, (i + 1) % count) for i in range(ends)])  84.9 us
    ppermute x26, starting transfers between devices, padded_2(): lax.ppermute(head, axis, [((i + 1) % count, i) for i in range(ends)])  62.8 us
    dot_general x6, matrix products, precond(): jnp.dot(scaled.astype(jnp.bfloat16), inverse_mat, preferred_element_type=...  29.9 us
    ppermute x26, waiting for transfers between devices, padded_2(): lax.ppermute(tail, axis, [(i, (i + 1) % count) for i in range(ends)])  29.5 us
  transfers between devices with their start and end apart: 54, of which 54 were waited for; matrix products, arithmetic and copies ran while one was open for 0% of the time, Pallas kernels for 0%

commit v1 on v0

--- a/solution.py
+++ b/solution.py
@@ -2,6 +2,7 @@
 import jax.numpy as jnp
 from jax import lax
 from jax.sharding import PartitionSpec as P
+from jax.lax import psum
 
 ITERS = 6
 
@@ -146,7 +147,9 @@
             jnp.dot(direction.astype(jnp.bfloat16), schur_mat, preferred_element_type=jnp.float32)
         )
         curv_local = jnp.sum(weight * direction * image, axis=1)
-        curv = lax.psum(curv_local, ("sx", "sy"))
+        curv = curv_local
+        for dd in ("sx", "sy"):
+            curv = psum(curv, dd)
         alpha = rz_now / curv
         solution_field = solution_field + alpha[:, None] * direction
         residual = residual - alpha[:, None] * image

time: 1440 us -> 1400 us (0.972)
  blocking collectives: 963 us -> 921 us
    psum x5 -> x12, blocking collectives: 340 us -> 310 us  [body(): curv = psum(curv, dd)]
where the time goes in v1:
time: 1400 us; the launch traced here: 1390 us
  blocking collectives  921 us (66%)
  waiting for transfers between devices  191 us (14%)
  starting transfers between devices  163 us (12%)
  matrix products  82.1 us (6%)
  other arithmetic  20.9 us (1%)
    psum x6, blocking collectives, products(): return lax.psum(jnp.sum(weight * left * right, axis=1), ('sx', 'sy'))  406 us
    psum x12, blocking collectives, body(): curv = psum(curv, dd)  310 us
    all_gather x6, blocking collectives, gather_coarse(): return lax.all_gather(coarse_local, ('sx', 'sy'), axis=0, tiled=True)  205 us
    ppermute x26, waiting for transfers between devices, padded_2(): lax.ppermute(head, axis, [((i + 1) % count, i) for i in range(ends)])  147 us
    ppermute x26, starting transfers between devices, padded_2(): lax.ppermute(tail, axis, [(i, (i + 1) % count) for i in range(ends)])  84.9 us
    ppermute x26, starting transfers between devices, padded_2(): lax.ppermute(head, axis, [((i + 1) % count, i) for i in range(ends)])  62.6 us
    dot_general x6, matrix products, precond(): jnp.dot(scaled.astype(jnp.bfloat16), inverse_mat, preferred_element_type=...  29.9 us
    ppermute x26, waiting for transfers between devices, padded_2(): lax.ppermute(tail, axis, [(i, (i + 1) % count) for i in range(ends)])  29.1 us
  transfers between devices with their start and end apart: 54, of which 54 were waited for; matrix products, arithmetic and copies ran while one was open for 0% of the time, Pallas kernels for 0%

profile of v1, /device:TPU:1, one launch (start us, length us, event | category | flops | bytes accessed | tf_op | source)
XLA Modules:
  0.0 1389.5 jit_solution(1930770638465826747)
XLA Ops:
  5.6 11.5 all-to-all-start
  32.6 8.1 all-to-all-done.1
  72.7 39.9 %all_gather.18 = f32[1024,64]{1,0:T(8,128)S(1)} all-gather(f32[8,64]{1,0:T(8,128)S(1)} %fusion.35), channel_id=1, replica_groups=mesh['sx'=16,'sy'=8] {'sx','sy'}, dimensions={0}, use_global_device_ids=true | all-gather | bytes 264192 | tf_op jit(solution)/shard_map/all_gather | solution.py:81
  136.0 7.7 collective-permute-done.7
  163.3 8.0 collective-permute-done.11
  172.5 32.7 %psum.127 = f32[64]{0:T(128)S(1)} all-reduce(f32[64]{0:T(128)S(1)} %get-tuple-element.2), channel_id=1, replica_groups=mesh['sx'=16,'sy'=8] {'sx'}, use_global_device_ids=true, to_apply=%region_9.10 | all-reduce | flops 64 | bytes 512 | tf_op jit(solution)/shard_map/psum | solution.py:152
  205.3 19.8 %psum.128 = f32[64]{0:T(128)S(1)} all-reduce(f32[64]{0:T(128)S(1)} %psum.127), channel_id=1, replica_groups=mesh['sx'=16,'sy'=8] {'sy'}, use_global_device_ids=true, to_apply=%region_10.11 | all-reduce | flops 64 | bytes 512 | tf_op jit(solution)/shard_map/psum | solution.py:152
  225.1 61.9 %psum.126 = f32[64]{0:T(128)S(1)} all-reduce(f32[64]{0:T(128)S(1)} %get-tuple-element.3), channel_id=1, replica_groups=mesh['sx'=16,'sy'=8] {'sx','sy'}, use_global_device_ids=true, to_apply=%region_7.8 | all-reduce | flops 64 | bytes 512 | tf_op jit(solution)/shard_map/psum | solution.py:137
  294.5 34.5 %all_gather.19 = f32[1024,64]{1,0:T(8,128)S(1)} all-gather(f32[8,64]{1,0:T(8,128)S(1)} %fusion.34), channel_id=1, replica_groups=mesh['sx'=16,'sy'=8] {'sx','sy'}, dimensions={0}, use_global_device_ids=true | all-gather | bytes 264192 | tf_op jit(solution)/shard_map/all_gather | solution.py:81
  347.2 7.7 collective-permute-done.15
  356.4 67.8 %psum.129 = f32[64]{0:T(128)S(1)} all-reduce(f32[64]{0:T(128)S(1)} %multiply_reduce_fusion.8), channel_id=1, replica_groups=mesh['sx'=16,'sy'=8] {'sx','sy'}, use_global_device_ids=true, to_apply=%region_12.13 | all-reduce | flops 64 | bytes 512 | tf_op jit(solution)/shard_map/psum | solution.py:137
  454.3 32.0 %psum.130 = f32[64]{0:T(128)S(1)} all-reduce(f32[64]{0:T(128)S(1)} %multiply_reduce_fusion.7), channel_id=1, replica_groups=mesh['sx'=16,'sy'=8] {'sx'}, use_global_device_ids=true, to_apply=%region_14.15 | all-reduce | flops 64 | bytes 512 | tf_op jit(solution)/shard_map/psum | solution.py:152
  486.3 19.5 %psum.131 = f32[64]{0:T(128)S(1)} all-reduce(f32[64]{0:T(128)S(1)} %psum.130), channel_id=1, replica_groups=mesh['sx'=16,'sy'=8] {'sy'}, use_global_device_ids=true, to_apply=%region_15.16 | all-reduce | flops 64 | bytes 512 | tf_op jit(solution)/shard_map/psum | solution.py:152
  513.1 32.6 %all_gather.20 = f32[1024,64]{1,0:T(8,128)S(1)} all-gather(f32[8,64]{1,0:T(8,128)S(1)} %fusion.33), channel_id=1, replica_groups=mesh['sx'=16,'sy'=8] {'sx','sy'}, dimensions={0}, use_global_device_ids=true | all-gather | bytes 264192 | tf_op jit(solution)/shard_map/all_gather | solution.py:81
  563.9 7.7 collective-permute-done.23
  573.9 69.1 %psum.132 = f32[64]{0:T(128)S(1)} all-reduce(f32[64]{0:T(128)S(1)} %multiply_reduce_fusion.6), channel_id=1, replica_groups=mesh['sx'=16,'sy'=8] {'sx','sy'}, use_global_device_ids=true, to_apply=%region_17.18 | all-reduce | flops 64 | bytes 512 | tf_op jit(solution)/shard_map/psum | solution.py:137
  674.0 32.0 %psum.133 = f32[64]{0:T(128)S(1)} all-reduce(f32[64]{0:T(128)S(1)} %multiply_reduce_fusion.5), channel_id=1, replica_groups=mesh['sx'=16,'sy'=8] {'sx'}, use_global_device_ids=true, to_apply=%region_19.20 | all-reduce | flops 64 | bytes 512 | tf_op jit(solution)/shard_map/psum | solution.py:152
  706.0 19.5 %psum.134 = f32[64]{0:T(128)S(1)} all-reduce(f32[64]{0:T(128)S(1)} %psum.133), channel_id=1, replica_groups=mesh['sx'=16,'sy'=8] {'sy'}, use_global_device_ids=true, to_apply=%region_20.21 | all-reduce | flops 64 | bytes 512 | tf_op jit(solution)/shard_map/psum | solution.py:152
  734.0 32.8 %all_gather.21 = f32[1024,64]{1,0:T(8,128)S(1)} all-gather(f32[8,64]{1,0:T(8,128)S(1)} %fusion.32), channel_id=1, replica_groups=mesh['sx'=16,'sy'=8] {'sx','sy'}, dimensions={0}, use_global_device_ids=true | all-gather | bytes 264192 | tf_op jit(solution)/shard_map/all_gather | solution.py:81
  785.0 7.7 collective-permute-done.31
  794.2 69.1 %psum.135 = f32[64]{0:T(128)S(1)} all-reduce(f32[64]{0:T(128)S(1)} %multiply_reduce_fusion.4), channel_id=1, replica_groups=mesh['sx'=16,'sy'=8] {'sx','sy'}, use_global_device_ids=true, to_apply=%region_22.23 | all-reduce | flops 64 | bytes 512 | tf_op jit(solution)/shard_map/psum | solution.py:137
  893.3 32.0 %psum.136 = f32[64]{0:T(128)S(1)} all-reduce(f32[64]{0:T(128)S(1)} %multiply_reduce_fusion.3), channel_id=1, replica_groups=mesh['sx'=16,'sy'=8] {'sx'}, use_global_device_ids=true, to_apply=%region_24.25 | all-reduce | flops 64 | bytes 512 | tf_op jit(solution)/shard_map/psum | solution.py:152
  925.3 19.5 %psum.137 = f32[64]{0:T(128)S(1)} all-reduce(f32[64]{0:T(128)S(1)} %psum.136), channel_id=1, replica_groups=mesh['sx'=16,'sy'=8] {'sy'}, use_global_device_ids=true, to_apply=%region_25.26 | all-reduce | flops 64 | bytes 512 | tf_op jit(solution)/shard_map/psum | solution.py:152
  952.2 32.5 %all_gather.22 = f32[1024,64]{1,0:T(8,128)S(1)} all-gather(f32[8,64]{1,0:T(8,128)S(1)} %fusion.31), channel_id=1, replica_groups=mesh['sx'=16,'sy'=8] {'sx','sy'}, dimensions={0}, use_global_device_ids=true | all-gather | bytes 264192 | tf_op jit(solution)/shard_map/all_gather | solution.py:81
  1002.9 7.7 collective-permute-done.39
  1012.9 69.1 %psum.138 = f32[64]{0:T(128)S(1)} all-reduce(f32[64]{0:T(128)S(1)} %multiply_reduce_fusion.2), channel_id=1, replica_groups=mesh['sx'=16,'sy'=8] {'sx','sy'}, use_global_device_ids=true, to_apply=%region_27.28 | all-reduce | flops 64 | bytes 512 | tf_op jit(solution)/shard_map/psum | solution.py:137
  1113.1 32.0 %psum.139 = f32[64]{0:T(128)S(1)} all-reduce(f32[64]{0:T(128)S(1)} %multiply_reduce_fusion.1), channel_id=1, replica_groups=mesh['sx'=16,'sy'=8] {'sx'}, use_global_device_ids=true, to_apply=%region_29.30 | all-reduce | flops 64 | bytes 512 | tf_op jit(solution)/shard_map/psum | solution.py:152
  1145.1 19.5 %psum.140 = f32[64]{0:T(128)S(1)} all-reduce(f32[64]{0:T(128)S(1)} %psum.139), channel_id=1, replica_groups=mesh['sx'=16,'sy'=8] {'sy'}, use_global_device_ids=true, to_apply=%region_30.31 | all-reduce | flops 64 | bytes 512 | tf_op jit(solution)/shard_map/psum | solution.py:152
  1172.0 32.6 %all_gather.23 = f32[1024,64]{1,0:T(8,128)S(1)} all-gather(f32[8,64]{1,0:T(8,128)S(1)} %fusion.30), channel_id=1, replica_groups=mesh['sx'=16,'sy'=8] {'sx','sy'}, dimensions={0}, use_global_device_ids=true | all-gather | bytes 264192 | tf_op jit(solution)/shard_map/all_gather | solution.py:81
  1232.0 69.1 %psum.141 = f32[64]{0:T(128)S(1)} all-reduce(f32[64]{0:T(128)S(1)} %multiply_reduce_fusion), channel_id=1, replica_groups=mesh['sx'=16,'sy'=8] {'sx','sy'}, use_global_device_ids=true, to_apply=%region_32.33 | all-reduce | flops 64 | bytes 512 | tf_op jit(solution)/shard_map/psum | solution.py:137
  1331.9 32.0 %psum.142 = f32[64]{0:T(128)S(1)} all-reduce(f32[64]{0:T(128)S(1)} %fusion.48), channel_id=1, replica_groups=mesh['sx'=16,'sy'=8] {'sx'}, use_global_device_ids=true, to_apply=%region_34.35 | all-reduce | flops 64 | bytes 512 | tf_op jit(solution)/shard_map/psum | solution.py:152
  1363.9 19.5 %psum.143 = f32[64]{0:T(128)S(1)} all-reduce(f32[64]{0:T(128)S(1)} %psum.142), channel_id=1, replica_groups=mesh['sx'=16,'sy'=8] {'sy'}, use_global_device_ids=true, to_apply=%region_35.36 | all-reduce | flops 64 | bytes 512 | tf_op jit(solution)/shard_map/psum | solution.py:152
  (323 shorter events, 400.2 us)
Async XLA Ops:
  5.6 21.0 %all-to-all-start = ((s32[128,1,4]{2,1,0:T(1,128)}), s32[128,1,4]{2,1,0:T(1,128)S(1)}, u32[]{:S(2)}, u32[]{:S(2)}) async-start(s32[128,1,4]{2,1,0:T(1,128)} %bitcast.7), calls=%async_computation | async-start | bytes 131072 | tf_op jit(solution)/shard_map/all_to_all | solution.py:109
  26.6 14.0 %all-to-all-start.1 = ((bf16[128,2,128]{2,1,0:T(2,128)(2,1)}), bf16[128,2,128]{2,1,0:T(2,128)(2,1)S(1)}, u32[]{:S(2)}, u32[]{:S(2)}) async-start(bf16[128,2,128]{2,1,0:T(2,128)(2,1)} %reshape.1414), calls=%async_computation.1 | async-start | bytes 131072 | tf_op jit(solution)/shard_map/all_to_all | solution.py:102
  53.7 14.6 %collective-permute-start.3 = (bf16[3,1,64,2048]{3,2,1,0:T(8,128)(2,1)S(1)}, bf16[3,1,64,2048]{3,2,1,0:T(8,128)(2,1)S(1)}, u32[]{:S(2)}, u32[]{:S(2)}) collective-permute-start(bf16[3,1,64,2048]{3,2,1,0:T(8,128)(2,1)S(1)} %pad_maximum_fusion), channel_id=1, source_target_pairs={{1,0},{2,1},{3,2},{4,3},{5,4},{6,5},{7,6},{9,8},{10,9},{11,10},{12... | collective-permute-start | bytes 2359304 | tf_op jit(solution)/shard_map/ppermute | solution.py:28
  57.6 11.9 collective-permute-start.2
  119.8 9.6 collective-permute-start.5
  130.4 13.3 collective-permute-start.7
  133.6 11.3 collective-permute-start.6
  156.1 15.3 %collective-permute-start.11 = (bf16[3,1,64,2048]{3,2,1,0:T(8,128)(2,1)S(1)}, bf16[3,1,64,2048]{3,2,1,0:T(8,128)(2,1)S(1)}, u32[]{:S(2)}, u32[]{:S(2)}) collective-permute-start(bf16[3,1,64,2048]{3,2,1,0:T(8,128)(2,1)S(1)} %pad_maximum_fusion.2), channel_id=1, source_target_pairs={{1,0},{2,1},{3,2},{4,3},{5,4},{6,5},{7,6},{9,8},{10,9},{11,10},{12... | collective-permute-start | bytes 2359304 | tf_op jit(solution)/shard_map/ppermute | solution.py:28
  158.0 14.2 %collective-permute-start.10 = (bf16[3,1,64,2048]{3,2,1,0:T(8,128)(2,1)S(1)}, bf16[3,1,64,2048]{3,2,1,0:T(8,128)(2,1)S(1)}, u32[]{:S(2)}, u32[]{:S(2)}) collective-permute-start(bf16[3,1,64,2048]{3,2,1,0:T(8,128)(2,1)S(1)} %pad_maximum_fusion.2), channel_id=1, source_target_pairs={{0,1},{1,2},{2,3},{3,4},{4,5},{5,6},{6,7},{8,9},{9,10},{10,11},{11... | collective-permute-start | bytes 2359304 | tf_op jit(solution)/shard_map/ppermute | solution.py:26
  331.0 9.6 collective-permute-start.13
  341.6 13.3 collective-permute-start.15
  344.8 11.3 collective-permute-start.14
  439.1 13.3 collective-permute-start.19
  443.2 10.8 collective-permute-start.18
  547.8 9.6 collective-permute-start.21
  558.4 13.3 collective-permute-start.23
  561.6 11.3 collective-permute-start.22
  658.7 13.4 collective-permute-start.27
  662.9 10.8 collective-permute-start.26
  768.8 9.6 collective-permute-start.29
  779.4 13.3 collective-permute-start.31
  782.6 11.3 collective-permute-start.30
  878.0 13.4 collective-permute-start.35
  882.2 10.8 collective-permute-start.34
  997.4 13.3 collective-permute-start.39
  1000.6 11.3 collective-permute-start.38
  1097.8 13.4 collective-permute-start.43
  1102.0 10.8 collective-permute-start.42
  1217.2 13.3 collective-permute-start.47
  1220.4 11.3 collective-permute-start.46
  1315.7 13.5 collective-permute-start.51
  1319.9 10.8 collective-permute-start.50
  (67 other events, 2574.9 us)
